TPU v7x, 32 devices: a whole 2x2x4 slice. The times are simulated.
32 devices in a mesh: parts: 2 (over y), aper: 4 (over z), rng: 2 (over x), sub: 2 (over core).
Axes of the slice: x: 2, y: 2, z: 4, core: 2. Of those that a mesh axis runs over, the one named last changes fastest.
Arguments:
- echoes: bfloat16 [2, 1024, 2048], P(None, ('parts', 'aper', 'sub'), 'rng'), parts along dimension 1, may hold values from -6 to 6
- chirp: bfloat16 [2, 512], replicated, may hold values from -0.1875 to 0.1875
- pulse_phase: float32 [1024, 64], P(('parts', 'aper', 'sub')), parts along dimension 0, may hold values from -3.140625 to 3.140625
- pulse_shift: int32 [1024, 64], P(('parts', 'aper', 'sub')), parts along dimension 0, may hold values from -8 to 8
- kernel_taps: int32 [2, 2, 8, 512], P(None, None, None, ('parts', 'aper', 'sub')), parts along dimension 3, may hold values from 0 to 31
- merge_shift: int32 [2, 2, 512], P(None, None, ('parts', 'aper', 'sub')), parts along dimension 2, may hold values from -8 to 8
- kernel_weights: float32 [2, 2, 2, 8, 512], P(None, None, None, None, ('parts', 'aper', 'sub')), parts along dimension 4, may hold values from -1 to 1
Outputs:
- image: bfloat16 [2, 512, 2048], P(None, ('parts', 'aper', 'sub'), 'rng'), parts along dimension 1
There are 2 independent parts, one for each index of `parts`. A program takes and returns all parts, laid end to end along the dimension named above; an argument that names none is the same for every part. Nothing has to cross between parts.
All inputs are finite; a program needn't handle non-finite values.
Results may differ from a plain program's by a relative error of at most 0.0099.
Values may be sent and summed in bfloat16 or wider, within the bound.
No kernel may reach another device: no remote copies, remote signals or barrier semaphores. Data moves between devices by JAX's collectives and lax.ppermute only.
A program may use at most 128 MiB of HBM per device.

v0:
```python
import math

import jax
import jax.numpy as jnp
from jax import lax
from jax.experimental import pallas as pl
from jax.experimental.pallas import tpu as pltpu
from jax.sharding import PartitionSpec as P

REACH = 8
BEAM_DEV = 32
PULSE_SUB = 128
LANES = 128
BLOCK = 256
F32 = jnp.float32
BF16 = jnp.bfloat16


def edge_mask(shape, slab):
    lane = lax.broadcasted_iota(jnp.int32, shape, 1)
    index = lax.axis_index("rng")
    last = lax.axis_size("rng") - 1
    right = jnp.where(index < last, 1, 0)
    left = jnp.where(index > 0, 1, 0)
    return jnp.where(lane < LANES // 2, right, left) > 0


def prepare_body(chirp, phase, shift, taps, mshift, mweight, toep, own, send, mats, rows, g_sc, m_sc, s_sc):
    tap_count = chirp.shape[1]
    span = toep.shape[1]
    for part in range(2):
        base = jnp.concatenate(
            [chirp[part : part + 1, :].astype(F32), jnp.zeros((1, span - tap_count), F32)], axis=1
        )
        skewed = pltpu.roll(jnp.broadcast_to(base, (BLOCK, span)), 0, 1, stride=1, stride_axis=0)
        toep[part] = skewed.T.astype(BF16)
    scale = 1.0 / math.sqrt(PULSE_SUB)
    angle = phase[...]
    real = jnp.cos(angle) * scale
    imag = jnp.sin(angle) * scale
    beams = angle.shape[1]
    top = jnp.concatenate([real, -imag], axis=0).T
    bottom = jnp.concatenate([imag, real], axis=0).T
    steps = shift[...].astype(F32)
    steps = jnp.concatenate([steps, steps], axis=0).T
    for half in range(beams // BEAM_DEV):
        at = slice(half * BEAM_DEV, (half + 1) * BEAM_DEV)
        g_sc[half] = jnp.concatenate([top[at], bottom[at], steps[at]], axis=0).astype(BF16)
    sub = lax.axis_index("sub")
    own[...] = g_sc[sub]
    send[...] = g_sc[1 - sub]
    aper = lax.axis_index("aper")
    beam = lax.broadcasted_iota(jnp.int32, (BEAM_DEV, 2 * BEAM_DEV), 0)
    for level in range(taps.shape[0]):
        for child in range(2):
            real_t = jnp.zeros((BEAM_DEV, 2 * BEAM_DEV), F32)
            imag_t = jnp.zeros((BEAM_DEV, 2 * BEAM_DEV), F32)
            tap = taps[level, child]
            tap = jnp.concatenate([tap, tap], axis=1)
            wr = mweight[0, level, child]
            wi = mweight[1, level, child]
            wre = jnp.concatenate([wr, wi], axis=1)
            wim = jnp.concatenate([-wi, wr], axis=1)
            for t in range(tap.shape[0]):
                hit = beam == tap[t : t + 1]
                real_t = real_t + jnp.where(hit, wre[t : t + 1], 0.0)
                imag_t = imag_t + jnp.where(hit, wim[t : t + 1], 0.0)
            m_sc[child] = jnp.concatenate([real_t, imag_t], axis=0).T.astype(BF16)
            step = mshift[level, child : child + 1].astype(F32)
            step = jnp.concatenate([step, step], axis=1)
            s_sc[child] = jnp.broadcast_to(step, (LANES, 2 * BEAM_DEV)).T.astype(jnp.int32)
        side = (aper >> level) & 1
        mats[level, 0] = m_sc[side]
        mats[level, 1] = m_sc[1 - side]
        rows[level, 0] = s_sc[side]
        rows[level, 1] = s_sc[1 - side]


def compress_body(echoes, right, left, toep, out):
    _, count, slab = echoes.shape
    span = toep.shape[1]
    reach = right.shape[2]
    index = lax.axis_index("rng")
    inner = echoes[...].reshape(2 * count, slab)
    right_on = jnp.where(index < lax.axis_size("rng") - 1, 1.0, 0.0).astype(BF16)
    left_on = jnp.where(index > 0, 1.0, 0.0).astype(BF16)
    after = right[...].reshape(2 * count, reach) * right_on
    before = left[:, :, left.shape[2] - LANES :].reshape(2 * count, LANES) * left_on
    ext = jnp.concatenate([inner, after], axis=1)
    blocks = slab // BLOCK
    stacked = jnp.concatenate(
        [ext[:, j * BLOCK : j * BLOCK + span] for j in range(blocks)], axis=0
    )
    by_real = jnp.dot(stacked, toep[0], preferred_element_type=F32)
    by_imag = jnp.dot(stacked, toep[1], preferred_element_type=F32)
    for j in range(blocks):
        a = slice(2 * count * j, 2 * count * j + count)
        b = slice(2 * count * j + count, 2 * count * (j + 1))
        at = slice(j * BLOCK, (j + 1) * BLOCK)
        out[:count, at] = (by_real[a] + by_imag[b]).astype(BF16)
        out[count:, at] = (by_real[b] - by_imag[a]).astype(BF16)
    need = span - BLOCK + LANES
    ends = jnp.concatenate(
        [
            ext[:, slab : slab + need],
            jnp.concatenate([before, ext[:, : need - LANES]], axis=1),
        ],
        axis=0,
    )
    by_real = jnp.dot(ends, toep[0, :need, :LANES], preferred_element_type=F32)
    by_imag = jnp.dot(ends, toep[1, :need, :LANES], preferred_element_type=F32)
    margins = []
    for side in range(2):
        a = slice(2 * count * side, 2 * count * side + count)
        b = slice(2 * count * side + count, 2 * count * (side + 1))
        margins.append(
            jnp.concatenate([by_real[a] + by_imag[b], by_real[b] - by_imag[a]], axis=0)
        )
    shape = margins[0].shape
    lane = lax.broadcasted_iota(jnp.int32, shape, 1)
    margin = jnp.where(lane < LANES // 2, margins[0], margins[1])
    out[:, slab:] = jnp.where(edge_mask(shape, slab), margin, 0.0).astype(BF16)


def project_body(own, other, mine, theirs, out, w_sc, y_sc):
    rows = 2 * BEAM_DEV
    width = out.shape[1]
    weight = jnp.concatenate([own[:rows, :], other[:rows, :]], axis=1)
    step = jnp.concatenate([own[rows:, :], other[rows:, :]], axis=1)
    step = jnp.concatenate([step, step], axis=0)
    offsets = range(-REACH, REACH + 1)
    for k, offset in enumerate(offsets):
        w_sc[k * rows : (k + 1) * rows, :] = jnp.where(
            step == jnp.asarray(offset, BF16), weight, jnp.zeros((), BF16)
        )
    pulses = jnp.concatenate([mine[...], theirs[...]], axis=0)
    y_sc[...] = jnp.dot(w_sc[...], pulses, preferred_element_type=F32)
    total = jnp.zeros((rows, width), F32)
    for k, offset in enumerate(offsets):
        part = y_sc[k * rows : (k + 1) * rows, :]
        total = total + (pltpu.roll(part, (-offset) % width, 1) if offset else part)
    slab = width - LANES
    out[:, :slab] = total[:, :slab].astype(BF16)
    margin = total[:, slab:]
    out[:, slab:] = jnp.where(edge_mask(margin.shape, slab), margin, 0.0).astype(BF16)


def shifted_rows(product, step):
    count = product.shape[1] // LANES
    lane = lax.broadcasted_iota(jnp.int32, step.shape, 1) + step
    index = lane & (LANES - 1)
    over = lane >= LANES
    under = lane < 0
    turned = [
        jnp.take_along_axis(product[:, i * LANES : (i + 1) * LANES], index, axis=1)
        for i in range(count)
    ]
    return [
        jnp.where(
            over, turned[(i + 1) % count], jnp.where(under, turned[(i - 1) % count], turned[i])
        )
        for i in range(count)
    ]


def merge_own_body(child, mats, rows, out, *, level):
    product = jnp.dot(mats[level, 0], child[...], preferred_element_type=F32)
    for i, tile in enumerate(shifted_rows(product, rows[level, 0])):
        out[:, i * LANES : (i + 1) * LANES] = tile


def merge_other_body(child, mats, rows, partial, out, *, level, last):
    product = jnp.dot(mats[level, 1], child[...], preferred_element_type=F32)
    tiles = shifted_rows(product, rows[level, 1])
    slab = child.shape[1] - LANES
    for i, tile in enumerate(tiles):
        at = slice(i * LANES, (i + 1) * LANES)
        value = partial[:, at] + tile
        if last:
            if i * LANES < slab:
                out[0, :, at] = value[:BEAM_DEV].astype(BF16)
                out[1, :, at] = value[BEAM_DEV:].astype(BF16)
        else:
            if i * LANES >= slab:
                value = jnp.where(edge_mask(value.shape, slab), value, 0.0)
            out[:, at] = value.astype(BF16)


def struct(shape, dtype):
    return jax.ShapeDtypeStruct(shape, dtype)


def neighbours(echoes, reach):
    slab = echoes.shape[2]
    size = lax.axis_size("rng")
    if size == 2 and slab >= reach:
        start = jnp.where(lax.axis_index("rng") == 0, slab - reach, 0)
        piece = lax.dynamic_slice_in_dim(echoes, start, reach, 2)
        got = lax.ppermute(piece, "rng", [(0, 1), (1, 0)])
        return got, got
    pieces = []
    distance = 1
    have = 0
    while have < reach:
        take = min(slab, reach - have)
        pairs = [(i, i - distance) for i in range(distance, size)]
        pieces.append(lax.ppermute(echoes[:, :, :take], "rng", pairs))
        have += take
        distance += 1
    pairs = [(i, i + 1) for i in range(size - 1)]
    left = lax.ppermute(echoes[:, :, slab - LANES :], "rng", pairs)
    return jnp.concatenate(pieces, axis=2), left


def shards(echoes, chirp, pulse_phase, pulse_shift, kernel_taps, merge_shift, kernel_weights):
    _, count, slab = echoes.shape
    tap_count = chirp.shape[1]
    levels = kernel_taps.shape[0]
    width = slab + LANES
    rows = 2 * BEAM_DEV
    span = tap_count + BLOCK
    right, left = neighbours(echoes, tap_count + LANES)
    table = (3 * BEAM_DEV, 2 * count)
    toep, own, send, mats, steps = pl.pallas_call(
        prepare_body,
        out_shape=(
            struct((2, span, BLOCK), BF16),
            struct(table, BF16),
            struct(table, BF16),
            struct((levels, 2, rows, rows), BF16),
            struct((levels, 2, rows, LANES), jnp.int32),
        ),
        scratch_shapes=[
            pltpu.VMEM((pulse_phase.shape[1] // BEAM_DEV,) + table, BF16),
            pltpu.VMEM((2, rows, rows), BF16),
            pltpu.VMEM((2, rows, LANES), jnp.int32),
        ],
        name="prepare",
    )(chirp, pulse_phase, pulse_shift, kernel_taps, merge_shift, kernel_weights)
    swap = [(0, 1), (1, 0)]
    other = lax.ppermute(send, "sub", swap)
    mine = pl.pallas_call(
        compress_body, out_shape=struct((2 * count, width), BF16), name="compress"
    )(echoes, right, left, toep)
    theirs = lax.ppermute(mine, "sub", swap)
    offsets = 2 * REACH + 1
    image = pl.pallas_call(
        project_body,
        out_shape=struct((rows, width), BF16),
        scratch_shapes=[
            pltpu.VMEM((offsets * rows, 4 * count), BF16),
            pltpu.VMEM((offsets * rows, width), F32),
        ],
        name="project",
    )(own, other, mine, theirs)
    size = lax.axis_size("aper")
    for level in range(levels):
        last = level == levels - 1
        pairs = [(i, i ^ (1 << level)) for i in range(size)]
        sibling = lax.ppermute(image, "aper", pairs)
        partial = pl.pallas_call(
            lambda *refs, level=level: merge_own_body(*refs, level=level),
            out_shape=struct((rows, width), F32),
            name="merge_own",
        )(image, mats, steps)
        image = pl.pallas_call(
            lambda *refs, level=level, last=last: merge_other_body(*refs, level=level, last=last),
            out_shape=struct((2, BEAM_DEV, slab) if last else (rows, width), BF16),
            name="merge_other",
        )(sibling, mats, steps, partial)
    return image


def solution(mesh):
    placed = (
        P(None, ("parts", "aper", "sub"), "rng"),
        P(),
        P(("parts", "aper", "sub"), None),
        P(("parts", "aper", "sub"), None),
        P(None, None, None, ("parts", "aper", "sub")),
        P(None, None, ("parts", "aper", "sub")),
        P(None, None, None, None, ("parts", "aper", "sub")),
    )
    return jax.shard_map(
        shards,
        mesh=mesh,
        in_specs=placed,
        out_specs=P(None, ("parts", "aper", "sub"), "rng"),
        check_vma=False,
    )
```

profile of v0, /device:TPU:0, one launch (start us, length us, event | category | flops | bytes accessed | tf_op | source)
XLA Modules:
  0.0 38.7 jit_solution(5340749298037285784)
XLA Ops:
  0.0 0.9 %constant_dynamic-slice_fusion = bf16[2,64,640]{2,1,0:T(8,128)(2,1)S(1)} fusion(bf16[2,64,1024]{2,1,0:T(8,128)(2,1)} %echoes.1, s32[]{:T(128)S(6)} %select_n.5), kind=kLoop, calls=%fused_computation | loop fusion | bytes 327684 | tf_op jit(solution)/shard_map/dynamic_slice | solution.py:198
  0.9 3.0 %collective-permute-start.1 = (bf16[2,64,640]{2,1,0:T(8,128)(2,1)S(1)}, bf16[2,64,640]{2,1,0:T(8,128)(2,1)S(1)}, u32[]{:S(2)}, u32[]{:S(2)}) collective-permute-start(bf16[2,64,640]{2,1,0:T(8,128)(2,1)S(1)} %constant_dynamic-slice_fusion), channel_id=1, source_target_pairs={{0,2},{2,0},{1,3},{3,1},{4,6},{6,4},{5,7},{7,5},{8,10},{10,8},{9,1... | collective-permute-start | bytes 491528 | tf_op jit(solution)/shard_map/ppermute | solution.py:199
  4.0 2.2 %prepare.1 = (bf16[2,768,256]{2,1,0:T(8,128)(2,1)}, bf16[96,128]{1,0:T(8,128)(2,1)}, bf16[96,128]{1,0:T(8,128)(2,1)}, bf16[2,2,64,64]{3,2,1,0:T(8,128)(2,1)}, s32[2,2,64,128]{3,2,1,0:T(8,128)}) custom-call(bf16[2,512]{1,0:T(2,128)(2,1)} %chirp.1, f32[64,64]{1,0:T(8,128)} %phase.1, s32[64,64]{1,0:T(8,128)} %shift.1, s32[2,2,8,32]{3,2,1,0:T(8,128)} %taps.1, ...), custom_call_target="tpu_custom_call" | custom-call | tf_op jit(solution)/shard_map/prepare/pallas_call | solution.py:224
  6.2 2.0 %collective-permute-done.1.right.left = bf16[2,64,640]{2,1,0:T(8,128)(2,1)S(1)} collective-permute-done((bf16[2,64,640]{2,1,0:T(8,128)(2,1)S(1)}, bf16[2,64,640]{2,1,0:T(8,128)(2,1)S(1)}, u32[]{:S(2)}, u32[]{:S(2)}) %collective-permute-start.1) | collective-permute-done | bytes 163872 | tf_op jit(solution)/shard_map/ppermute | solution.py:199
  8.2 0.0 copy-start
  8.2 0.7 %copy-done = bf16[2,64,640]{2,1,0:T(8,128)(2,1)} copy-done((bf16[2,64,640]{2,1,0:T(8,128)(2,1)}, bf16[2,64,640]{2,1,0:T(8,128)(2,1)S(1)}, u32[]{:S(2)}) %copy-start) | copy-done | bytes 163864
  8.8 0.0 copy-start.5
  8.8 2.9 %compress.1.mine = bf16[128,1152]{1,0:T(8,128)(2,1)} custom-call(bf16[2,64,1024]{2,1,0:T(8,128)(2,1)} %echoes.1, bf16[2,64,640]{2,1,0:T(8,128)(2,1)} %copy-done, bf16[2,64,640]{2,1,0:T(8,128)(2,1)} %copy-done, bf16[2,768,256]{2,1,0:T(8,128)(2,1)} %get-tuple-element.12.toep), custom_call_target="tpu_custom_call" | custom-call | tf_op jit(solution)/shard_map/compress/pallas_call | solution.py:242
  11.7 0.0 collective-permute-start.2
  11.7 0.0 copy-done.5
  11.7 0.5 %collective-permute-start = (bf16[96,128]{1,0:T(8,128)(2,1)S(1)}, bf16[96,128]{1,0:T(8,128)(2,1)S(1)}, u32[]{:S(2)}, u32[]{:S(2)}) collective-permute-start(bf16[96,128]{1,0:T(8,128)(2,1)S(1)} %copy-done.5), channel_id=1, source_target_pairs={{0,1},{1,0},{2,3},{3,2},{4,5},{5,4},{6,7},{7,6},{8,9},{9,8},{10,11... | collective-permute-start | bytes 73736 | tf_op jit(solution)/shard_map/ppermute | solution.py:241
  12.2 1.3 %collective-permute-done.other = bf16[96,128]{1,0:T(8,128)(2,1)S(1)} collective-permute-done((bf16[96,128]{1,0:T(8,128)(2,1)S(1)}, bf16[96,128]{1,0:T(8,128)(2,1)S(1)}, u32[]{:S(2)}, u32[]{:S(2)}) %collective-permute-start) | collective-permute-done | bytes 24608 | tf_op jit(solution)/shard_map/ppermute | solution.py:241
  13.5 0.0 copy-start.4
  13.5 0.0 collective-permute-done.2.theirs
  13.5 0.0 copy-start.1
  13.5 0.6 %copy-done.4 = bf16[96,128]{1,0:T(8,128)(2,1)} copy-done((bf16[96,128]{1,0:T(8,128)(2,1)}, bf16[96,128]{1,0:T(8,128)(2,1)S(1)}, u32[]{:S(2)}) %copy-start.4) | copy-done | bytes 24600
  14.1 0.1 copy-done.1
  14.2 3.3 %project.1.refs_0_ = bf16[64,1152]{1,0:T(8,128)(2,1)} custom-call(bf16[96,128]{1,0:T(8,128)(2,1)} %get-tuple-element.10.own, bf16[96,128]{1,0:T(8,128)(2,1)} %copy-done.4, bf16[128,1152]{1,0:T(8,128)(2,1)} %compress.1.mine, bf16[128,1152]{1,0:T(8,128)(2,1)} %copy-done.1), custom_call_target="tpu_custom_call" | custom-call | tf_op jit(solution)/shard_map/project/pallas_call | solution.py:247
  17.5 1.8 %collective-permute-start.3 = (bf16[64,1152]{1,0:T(8,128)(2,1)}, bf16[64,1152]{1,0:T(8,128)(2,1)S(1)}, u32[]{:S(2)}, u32[]{:S(2)}) collective-permute-start(bf16[64,1152]{1,0:T(8,128)(2,1)} %project.1.refs_0_), channel_id=1, source_target_pairs={{0,4},{4,0},{8,12},{12,8},{1,5},{5,1},{9,13},{13,9},{2,6},{6,2},{1... | collective-permute-start | bytes 442376 | tf_op jit(solution)/shard_map/ppermute | solution.py:260
  19.3 2.1 %merge_own.2.refs_3_ = f32[64,1152]{1,0:T(8,128)} custom-call(bf16[64,1152]{1,0:T(8,128)(2,1)} %project.1.refs_0_, bf16[2,2,64,64]{3,2,1,0:T(8,128)(2,1)} %get-tuple-element.13.refs_1_, s32[2,2,64,128]{3,2,1,0:T(8,128)} %get-tuple-element.14.refs_2_), custom_call_target="tpu_custom_call" | custom-call | tf_op jit(solution)/shard_map/merge_own/pallas_call | solution.py:261
  21.4 2.3 %collective-permute-done.3.refs_0_ = bf16[64,1152]{1,0:T(8,128)(2,1)S(1)} collective-permute-done((bf16[64,1152]{1,0:T(8,128)(2,1)}, bf16[64,1152]{1,0:T(8,128)(2,1)S(1)}, u32[]{:S(2)}, u32[]{:S(2)}) %collective-permute-start.3) | collective-permute-done | bytes 147488 | tf_op jit(solution)/shard_map/ppermute | solution.py:260
  23.7 0.0 copy-start.3
  23.7 0.6 %copy-done.3 = bf16[64,1152]{1,0:T(8,128)(2,1)} copy-done((bf16[64,1152]{1,0:T(8,128)(2,1)}, bf16[64,1152]{1,0:T(8,128)(2,1)S(1)}, u32[]{:S(2)}) %copy-start.3) | copy-done | bytes 147480
  24.3 2.1 %merge_other.2.refs_0_ = bf16[64,1152]{1,0:T(8,128)(2,1)} custom-call(bf16[64,1152]{1,0:T(8,128)(2,1)} %copy-done.3, bf16[2,2,64,64]{3,2,1,0:T(8,128)(2,1)} %get-tuple-element.13.refs_1_, s32[2,2,64,128]{3,2,1,0:T(8,128)} %get-tuple-element.14.refs_2_, f32[64,1152]{1,0:T(8,128)} %merge_own.2.refs_3_), custom_call_target="tpu_custom_call" | custom-call | tf_op jit(solution)/shard_map/merge_other/pallas_call | solution.py:266
  26.5 2.8 %collective-permute-start.4 = (bf16[64,1152]{1,0:T(8,128)(2,1)}, bf16[64,1152]{1,0:T(8,128)(2,1)S(1)}, u32[]{:S(2)}, u32[]{:S(2)}) collective-permute-start(bf16[64,1152]{1,0:T(8,128)(2,1)} %merge_other.2.refs_0_), channel_id=1, source_target_pairs={{0,8},{4,12},{8,0},{12,4},{1,9},{5,13},{9,1},{13,5},{2,10},{6,14},... | collective-permute-start | bytes 442376 | tf_op jit(solution)/shard_map/ppermute | solution.py:260
  29.2 2.1 %merge_own.3.refs_3_ = f32[64,1152]{1,0:T(8,128)} custom-call(bf16[64,1152]{1,0:T(8,128)(2,1)} %merge_other.2.refs_0_, bf16[2,2,64,64]{3,2,1,0:T(8,128)(2,1)} %get-tuple-element.13.refs_1_, s32[2,2,64,128]{3,2,1,0:T(8,128)} %get-tuple-element.14.refs_2_), custom_call_target="tpu_custom_call" | custom-call | tf_op jit(solution)/shard_map/merge_own/pallas_call | solution.py:261
  31.3 4.6 %collective-permute-done.4.refs_0_ = bf16[64,1152]{1,0:T(8,128)(2,1)S(1)} collective-permute-done((bf16[64,1152]{1,0:T(8,128)(2,1)}, bf16[64,1152]{1,0:T(8,128)(2,1)S(1)}, u32[]{:S(2)}, u32[]{:S(2)}) %collective-permute-start.4) | collective-permute-done | bytes 147488 | tf_op jit(solution)/shard_map/ppermute | solution.py:260
  35.9 0.0 copy-start.2
  35.9 0.7 %copy-done.2 = bf16[64,1152]{1,0:T(8,128)(2,1)} copy-done((bf16[64,1152]{1,0:T(8,128)(2,1)}, bf16[64,1152]{1,0:T(8,128)(2,1)S(1)}, u32[]{:S(2)}) %copy-start.2) | copy-done | bytes 147480
  36.5 2.1 %merge_other.3 = bf16[2,32,1024]{2,1,0:T(8,128)(2,1)} custom-call(bf16[64,1152]{1,0:T(8,128)(2,1)} %copy-done.2, bf16[2,2,64,64]{3,2,1,0:T(8,128)(2,1)} %get-tuple-element.13.refs_1_, s32[2,2,64,128]{3,2,1,0:T(8,128)} %get-tuple-element.14.refs_2_, f32[64,1152]{1,0:T(8,128)} %merge_own.3.refs_3_), custom_call_target="tpu_custom_call" | custom-call | tf_op jit(solution)/shard_map/merge_other/pallas_call | solution.py:266
Async XLA Ops:
  0.9 7.2 %collective-permute-start.1 = (bf16[2,64,640]{2,1,0:T(8,128)(2,1)S(1)}, bf16[2,64,640]{2,1,0:T(8,128)(2,1)S(1)}, u32[]{:S(2)}, u32[]{:S(2)}) collective-permute-start(bf16[2,64,640]{2,1,0:T(8,128)(2,1)S(1)} %constant_dynamic-slice_fusion), channel_id=1, source_target_pairs={{0,2},{2,0},{1,3},{3,1},{4,6},{6,4},{5,7},{7,5},{8,10},{10,8},{9,1... | collective-permute-start | bytes 491528 | tf_op jit(solution)/shard_map/ppermute | solution.py:199
  8.2 0.7 %copy-start = (bf16[2,64,640]{2,1,0:T(8,128)(2,1)}, bf16[2,64,640]{2,1,0:T(8,128)(2,1)S(1)}, u32[]{:S(2)}) copy-start(bf16[2,64,640]{2,1,0:T(8,128)(2,1)S(1)} %collective-permute-done.1.right.left) | copy-start | bytes 491524
  8.8 2.9 %copy-start.5 = (bf16[96,128]{1,0:T(8,128)(2,1)S(1)}, bf16[96,128]{1,0:T(8,128)(2,1)}, u32[]{:S(2)}) copy-start(bf16[96,128]{1,0:T(8,128)(2,1)} %get-tuple-element.11) | copy-start | bytes 73732
  11.7 1.8 %collective-permute-start.2 = (bf16[128,1152]{1,0:T(8,128)(2,1)}, bf16[128,1152]{1,0:T(8,128)(2,1)S(1)}, u32[]{:S(2)}, u32[]{:S(2)}) collective-permute-start(bf16[128,1152]{1,0:T(8,128)(2,1)} %compress.1.mine), channel_id=1, source_target_pairs={{0,1},{1,0},{2,3},{3,2},{4,5},{5,4},{6,7},{7,6},{8,9},{9,8},{10,11... | collective-permute-start | bytes 884744 | tf_op jit(solution)/shard_map/ppermute | solution.py:245
  11.7 1.8 %collective-permute-start = (bf16[96,128]{1,0:T(8,128)(2,1)S(1)}, bf16[96,128]{1,0:T(8,128)(2,1)S(1)}, u32[]{:S(2)}, u32[]{:S(2)}) collective-permute-start(bf16[96,128]{1,0:T(8,128)(2,1)S(1)} %copy-done.5), channel_id=1, source_target_pairs={{0,1},{1,0},{2,3},{3,2},{4,5},{5,4},{6,7},{7,6},{8,9},{9,8},{10,11... | collective-permute-start | bytes 73736 | tf_op jit(solution)/shard_map/ppermute | solution.py:241
  13.5 0.6 %copy-start.4 = (bf16[96,128]{1,0:T(8,128)(2,1)}, bf16[96,128]{1,0:T(8,128)(2,1)S(1)}, u32[]{:S(2)}) copy-start(bf16[96,128]{1,0:T(8,128)(2,1)S(1)} %collective-permute-done.other) | copy-start | bytes 73732
  13.5 0.7 %copy-start.1 = (bf16[128,1152]{1,0:T(8,128)(2,1)}, bf16[128,1152]{1,0:T(8,128)(2,1)S(1)}, u32[]{:S(2)}) copy-start(bf16[128,1152]{1,0:T(8,128)(2,1)S(1)} %collective-permute-done.2.theirs) | copy-start | bytes 884740
  17.5 6.2 %collective-permute-start.3 = (bf16[64,1152]{1,0:T(8,128)(2,1)}, bf16[64,1152]{1,0:T(8,128)(2,1)S(1)}, u32[]{:S(2)}, u32[]{:S(2)}) collective-permute-start(bf16[64,1152]{1,0:T(8,128)(2,1)} %project.1.refs_0_), channel_id=1, source_target_pairs={{0,4},{4,0},{8,12},{12,8},{1,5},{5,1},{9,13},{13,9},{2,6},{6,2},{1... | collective-permute-start | bytes 442376 | tf_op jit(solution)/shard_map/ppermute | solution.py:260
  23.7 0.6 %copy-start.3 = (bf16[64,1152]{1,0:T(8,128)(2,1)}, bf16[64,1152]{1,0:T(8,128)(2,1)S(1)}, u32[]{:S(2)}) copy-start(bf16[64,1152]{1,0:T(8,128)(2,1)S(1)} %collective-permute-done.3.refs_0_) | copy-start | bytes 442372
  26.5 9.4 %collective-permute-start.4 = (bf16[64,1152]{1,0:T(8,128)(2,1)}, bf16[64,1152]{1,0:T(8,128)(2,1)S(1)}, u32[]{:S(2)}, u32[]{:S(2)}) collective-permute-start(bf16[64,1152]{1,0:T(8,128)(2,1)} %merge_other.2.refs_0_), channel_id=1, source_target_pairs={{0,8},{4,12},{8,0},{12,4},{1,9},{5,13},{9,1},{13,5},{2,10},{6,14},... | collective-permute-start | bytes 442376 | tf_op jit(solution)/shard_map/ppermute | solution.py:260
  35.9 0.7 %copy-start.2 = (bf16[64,1152]{1,0:T(8,128)(2,1)}, bf16[64,1152]{1,0:T(8,128)(2,1)S(1)}, u32[]{:S(2)}) copy-start(bf16[64,1152]{1,0:T(8,128)(2,1)S(1)} %collective-permute-done.4.refs_0_) | copy-start | bytes 442372
where the time goes:
time: 39 us; the launch traced here: 38.7 us
  Pallas kernels  16.8 us (43%)
  waiting for transfers between devices  10.2 us (26%)
  starting transfers between devices  8.11 us (21%)
  local copies, waits for them, and re-layouts  3.61 us (9%)
    ppermute x2, waiting for transfers between devices, shards(): sibling = lax.ppermute(image, 'aper', pairs)  6.9 us
    ppermute x2, starting transfers between devices, shards(): sibling = lax.ppermute(image, 'aper', pairs)  4.57 us
    pallas_call x2, Pallas kernels, shards(): pl.pallas_call(lambda *refs, level=level, last=last: merge_other_body(*re...  4.27 us
    pallas_call x2, Pallas kernels, shards(): pl.pallas_call(lambda *refs, level=level: merge_own_body(*refs, level=lev...  4.12 us
    pallas_call x1, Pallas kernels, shards(): pl.pallas_call(project_body, out_shape=struct((rows, width), BF16), scrat...  3.26 us
    ppermute x1, starting transfers between devices, neighbours(): got = lax.ppermute(piece, 'rng', [(0, 1), (1, 0)])  3.03 us
    pallas_call x1, Pallas kernels, shards(): pl.pallas_call(compress_body, out_shape=struct((2 * count, width), BF16),...  2.87 us
    unnamed x12, local copies, waits for them, and re-layouts  2.68 us
  transfers between devices with their start and end apart: 5, of which 4 were waited for; matrix products, arithmetic and copies ran while one was open for 0% of the time, Pallas kernels for 16%

commit v1 on v0

--- a/solution.py
+++ b/solution.py
@@ -1,3 +1,4 @@
+import functools
 import math
 
 import jax
@@ -190,6 +191,19 @@
     return jax.ShapeDtypeStruct(shape, dtype)
 
 
+def local_call(body, args, out_shape, name, limit, scratch=()):
+    vmem = pl.BlockSpec(memory_space=pltpu.VMEM)
+    return pl.pallas_call(
+        body,
+        out_shape=out_shape,
+        in_specs=[vmem] * len(args),
+        out_specs=jax.tree.map(lambda _: vmem, out_shape),
+        scratch_shapes=list(scratch),
+        compiler_params=pltpu.CompilerParams(vmem_limit_bytes=limit),
+        name=name,
+    )(*args)
+
+
 def neighbours(echoes, reach):
     slab = echoes.shape[2]
     size = lax.axis_size("rng")
@@ -221,53 +235,65 @@
     span = tap_count + BLOCK
     right, left = neighbours(echoes, tap_count + LANES)
     table = (3 * BEAM_DEV, 2 * count)
-    toep, own, send, mats, steps = pl.pallas_call(
+    toep, own, send, mats, steps = local_call(
         prepare_body,
-        out_shape=(
+        (chirp, pulse_phase, pulse_shift, kernel_taps, merge_shift, kernel_weights),
+        (
             struct((2, span, BLOCK), BF16),
             struct(table, BF16),
             struct(table, BF16),
             struct((levels, 2, rows, rows), BF16),
             struct((levels, 2, rows, LANES), jnp.int32),
         ),
-        scratch_shapes=[
+        "prepare",
+        8 << 20,
+        (
             pltpu.VMEM((pulse_phase.shape[1] // BEAM_DEV,) + table, BF16),
             pltpu.VMEM((2, rows, rows), BF16),
             pltpu.VMEM((2, rows, LANES), jnp.int32),
-        ],
-        name="prepare",
-    )(chirp, pulse_phase, pulse_shift, kernel_taps, merge_shift, kernel_weights)
+        ),
+    )
     swap = [(0, 1), (1, 0)]
     other = lax.ppermute(send, "sub", swap)
-    mine = pl.pallas_call(
-        compress_body, out_shape=struct((2 * count, width), BF16), name="compress"
-    )(echoes, right, left, toep)
+    mine = local_call(
+        compress_body,
+        (echoes, right, left, toep),
+        struct((2 * count, width), BF16),
+        "compress",
+        16 << 20,
+    )
     theirs = lax.ppermute(mine, "sub", swap)
     offsets = 2 * REACH + 1
-    image = pl.pallas_call(
+    image = local_call(
         project_body,
-        out_shape=struct((rows, width), BF16),
-        scratch_shapes=[
+        (own, other, mine, theirs),
+        struct((rows, width), BF16),
+        "project",
+        16 << 20,
+        (
             pltpu.VMEM((offsets * rows, 4 * count), BF16),
             pltpu.VMEM((offsets * rows, width), F32),
-        ],
-        name="project",
-    )(own, other, mine, theirs)
+        ),
+    )
     size = lax.axis_size("aper")
     for level in range(levels):
         last = level == levels - 1
         pairs = [(i, i ^ (1 << level)) for i in range(size)]
         sibling = lax.ppermute(image, "aper", pairs)
-        partial = pl.pallas_call(
-            lambda *refs, level=level: merge_own_body(*refs, level=level),
-            out_shape=struct((rows, width), F32),
-            name="merge_own",
-        )(image, mats, steps)
-        image = pl.pallas_call(
-            lambda *refs, level=level, last=last: merge_other_body(*refs, level=level, last=last),
-            out_shape=struct((2, BEAM_DEV, slab) if last else (rows, width), BF16),
-            name="merge_other",
-        )(sibling, mats, steps, partial)
+        partial = local_call(
+            functools.partial(merge_own_body, level=level),
+            (image, mats, steps),
+            struct((rows, width), F32),
+            "merge_own",
+            4 << 20,
+        )
+        image = local_call(
+            functools.partial(merge_other_body, level=level, last=last),
+            (sibling, mats, steps, partial),
+            struct((2, BEAM_DEV, slab) if last else (rows, width), BF16),
+            "merge_other",
+            4 << 20,
+        )
     return image
 
 

time: 39 us -> 29.1 us (0.75)
  Pallas kernels: 16.8 us -> 4.88 us
  waiting for transfers between devices: 10.2 us -> 13.1 us
  local copies, waits for them, and re-layouts: 3.61 us -> 2.48 us
    pallas_call x7, Pallas kernels: 16.8 us -> 4.88 us  [local_call(): pl.pallas_call(body, out_shape=out_shape, in_specs=[vmem] * len(args), ou...]
    ppermute x2, waiting for transfers between devices: 6.9 us -> 9.91 us  [shards(): sibling = lax.ppermute(image, 'aper', pairs)]
    unnamed x12 -> x14, local copies, waits for them, and re-layouts: 2.68 us -> 1.49 us
  transfers between devices with their start and end apart: 5 -> 5, of which waited for: 4 -> 4; matrix products, arithmetic and copies ran while one was open for 0% -> 0% of each run, Pallas kernels for 16% -> 4%
where the time goes in v1:
time: 29.1 us; the launch traced here: 28.9 us
  waiting for transfers between devices  13.1 us (45%)
  starting transfers between devices  8.31 us (29%)
  Pallas kernels  4.88 us (17%)
  local copies, waits for them, and re-layouts  2.48 us (9%)
    ppermute x2, waiting for transfers between devices, shards(): sibling = lax.ppermute(image, 'aper', pairs)  9.91 us
    pallas_call x7, Pallas kernels, local_call(): pl.pallas_call(body, out_shape=out_shape, in_specs=[vmem] * len(args), ou...  4.88 us
    ppermute x2, starting transfers between devices, shards(): sibling = lax.ppermute(image, 'aper', pairs)  4.71 us
    ppermute x1, starting transfers between devices, neighbours(): got = lax.ppermute(piece, 'rng', [(0, 1), (1, 0)])  3.03 us
    ppermute x1, waiting for transfers between devices, neighbours(): got = lax.ppermute(piece, 'rng', [(0, 1), (1, 0)])  2.11 us
    unnamed x14, local copies, waits for them, and re-layouts  1.49 us
    ppermute x1, waiting for transfers between devices, shards(): other = lax.ppermute(send, 'sub', swap)  1.11 us
    dynamic_slice x1, local copies, waits for them, and re-layouts, neighbours(): piece = lax.dynamic_slice_in_dim(echoes, start, reach, 2)  0.99 us
  transfers between devices with their start and end apart: 5, of which 4 were waited for; matrix products, arithmetic and copies ran while one was open for 0% of the time, Pallas kernels for 4%

profile of v1, /device:TPU:0, one launch (start us, length us, event | category | flops | bytes accessed | tf_op | source)
XLA Modules:
  0.0 28.9 jit_solution(671745342310617034)
XLA Ops:
  0.0 0.0 copy-start
  0.0 0.0 copy-start.1
  0.0 0.0 copy-start.2
  0.0 0.0 copy-start.5
  0.0 0.0 copy-start.6
  0.0 1.0 %constant_dynamic-slice_fusion = bf16[2,64,640]{2,1,0:T(8,128)(2,1)S(1)} fusion(bf16[2,64,1024]{2,1,0:T(8,128)(2,1)} %echoes.1, s32[]{:T(128)S(6)} %select_n.5), kind=kLoop, calls=%fused_computation | loop fusion | bytes 327684 | tf_op jit(solution)/shard_map/dynamic_slice | solution.py:212
  1.0 3.0 %collective-permute-start.1 = (bf16[2,64,640]{2,1,0:T(8,128)(2,1)S(1)}, bf16[2,64,640]{2,1,0:T(8,128)(2,1)S(1)}, u32[]{:S(2)}, u32[]{:S(2)}) collective-permute-start(bf16[2,64,640]{2,1,0:T(8,128)(2,1)S(1)} %constant_dynamic-slice_fusion), channel_id=1, source_target_pairs={{0,2},{2,0},{1,3},{3,1},{4,6},{6,4},{5,7},{7,5},{8,10},{10,8},{9,1... | collective-permute-start | bytes 491528 | tf_op jit(solution)/shard_map/ppermute | solution.py:213
  4.0 0.0 copy-done.1
  4.0 0.0 copy-done.2
  4.0 0.0 copy-done.5
  4.0 0.0 copy-done.6
  4.1 0.0 copy-start.3
  4.1 0.7 %copy-done.3 = f32[2,2,2,8,32]{4,3,2,1,0:T(8,128)S(1)} copy-done((f32[2,2,2,8,32]{4,3,2,1,0:T(8,128)S(1)}, f32[2,2,2,8,32]{4,3,2,1,0:T(8,128)}, u32[]{:S(2)}) %copy-start.3) | copy-done | bytes 8216
  4.8 0.0 copy-start.4
  4.8 0.7 %copy-done.4 = s32[2,2,8,32]{3,2,1,0:T(8,128)S(1)} copy-done((s32[2,2,8,32]{3,2,1,0:T(8,128)S(1)}, s32[2,2,8,32]{3,2,1,0:T(8,128)}, u32[]{:S(2)}) %copy-start.4) | copy-done | bytes 4120
  5.5 0.6 %prepare.1 = (bf16[2,768,256]{2,1,0:T(8,128)(2,1)S(1)}, bf16[96,128]{1,0:T(8,128)(2,1)S(1)}, bf16[96,128]{1,0:T(8,128)(2,1)S(1)}, bf16[2,2,64,64]{3,2,1,0:T(8,128)(2,1)S(1)}, s32[2,2,64,128]{3,2,1,0:T(8,128)S(1)}) custom-call(bf16[2,512]{1,0:T(2,128)(2,1)S(1)} %copy-done.5, f32[64,64]{1,0:T(8,128)S(1)} %copy-done.1, s32[64,64]{1,0:T(8,128)S(1)} %copy-done.2, ...), custom_call_target="tpu_custom_call" | custom-call | tf_op jit(solution)/shard_map/prepare/pallas_call | solution.py:196
  6.1 2.1 %collective-permute-done.1.right.left = bf16[2,64,640]{2,1,0:T(8,128)(2,1)S(1)} collective-permute-done((bf16[2,64,640]{2,1,0:T(8,128)(2,1)S(1)}, bf16[2,64,640]{2,1,0:T(8,128)(2,1)S(1)}, u32[]{:S(2)}, u32[]{:S(2)}) %collective-permute-start.1) | collective-permute-done | bytes 163872 | tf_op jit(solution)/shard_map/ppermute | solution.py:213
  8.2 0.0 copy-done
  8.2 0.8 %compress.1.mine = bf16[128,1152]{1,0:T(8,128)(2,1)S(1)} custom-call(bf16[2,64,1024]{2,1,0:T(8,128)(2,1)S(1)} %copy-done, bf16[2,64,640]{2,1,0:T(8,128)(2,1)S(1)} %collective-permute-done.1.right.left, bf16[2,64,640]{2,1,0:T(8,128)(2,1)S(1)} %collective-permute-done.1.right.left, bf16[2,768,256]{2,1,0:T(8,128)(2,1)S(1)} %get-tuple-element.12.toep), custom_call_target="tpu_custom_call" | custom-call | tf_op jit(solution)/shard_map/compress/pallas_call | solution.py:196
  9.0 0.1 collective-permute-start.2
  9.1 0.5 %collective-permute-start = (bf16[96,128]{1,0:T(8,128)(2,1)S(1)}, bf16[96,128]{1,0:T(8,128)(2,1)S(1)}, u32[]{:S(2)}, u32[]{:S(2)}) collective-permute-start(bf16[96,128]{1,0:T(8,128)(2,1)S(1)} %get-tuple-element.11), channel_id=1, source_target_pairs={{0,1},{1,0},{2,3},{3,2},{4,5},{5,4},{6,7},{7,6},{8,9},{9,8},{10,11... | collective-permute-start | bytes 73736 | tf_op jit(solution)/shard_map/ppermute | solution.py:257
  9.6 1.1 %collective-permute-done.other = bf16[96,128]{1,0:T(8,128)(2,1)S(1)} collective-permute-done((bf16[96,128]{1,0:T(8,128)(2,1)S(1)}, bf16[96,128]{1,0:T(8,128)(2,1)S(1)}, u32[]{:S(2)}, u32[]{:S(2)}) %collective-permute-start) | collective-permute-done | bytes 24608 | tf_op jit(solution)/shard_map/ppermute | solution.py:257
  10.7 0.0 collective-permute-done.2.theirs
  10.7 1.5 %project.1.child = bf16[64,1152]{1,0:T(8,128)(2,1)S(1)} custom-call(bf16[96,128]{1,0:T(8,128)(2,1)S(1)} %get-tuple-element.10.own, bf16[96,128]{1,0:T(8,128)(2,1)S(1)} %collective-permute-done.other, bf16[128,1152]{1,0:T(8,128)(2,1)S(1)} %compress.1.mine, bf16[128,1152]{1,0:T(8,128)(2,1)S(1)} %collective-permute-done.2.theirs), custom_call_target="tpu_custom_call" | custom-call | tf_op jit(solution)/shard_map/project/pallas_call | solution.py:196
  12.2 1.9 %collective-permute-start.3 = (bf16[64,1152]{1,0:T(8,128)(2,1)S(1)}, bf16[64,1152]{1,0:T(8,128)(2,1)S(1)}, u32[]{:S(2)}, u32[]{:S(2)}) collective-permute-start(bf16[64,1152]{1,0:T(8,128)(2,1)S(1)} %project.1.child), channel_id=1, source_target_pairs={{0,4},{4,0},{8,12},{12,8},{1,5},{5,1},{9,13},{13,9},{2,6},{6,2},{1... | collective-permute-start | bytes 442376 | tf_op jit(solution)/shard_map/ppermute | solution.py:282
  14.1 0.3 %merge_own.2.partial = f32[64,1152]{1,0:T(8,128)S(1)} custom-call(bf16[64,1152]{1,0:T(8,128)(2,1)S(1)} %project.1.child, bf16[2,2,64,64]{3,2,1,0:T(8,128)(2,1)S(1)} %get-tuple-element.13.mats, s32[2,2,64,128]{3,2,1,0:T(8,128)S(1)} %get-tuple-element.14.rows), custom_call_target="tpu_custom_call" | custom-call | tf_op jit(solution)/shard_map/merge_own/pallas_call | solution.py:196
  14.4 3.8 %collective-permute-done.3.child = bf16[64,1152]{1,0:T(8,128)(2,1)S(1)} collective-permute-done((bf16[64,1152]{1,0:T(8,128)(2,1)S(1)}, bf16[64,1152]{1,0:T(8,128)(2,1)S(1)}, u32[]{:S(2)}, u32[]{:S(2)}) %collective-permute-start.3) | collective-permute-done | bytes 147488 | tf_op jit(solution)/shard_map/ppermute | solution.py:282
  18.2 0.3 %merge_other.2.child = bf16[64,1152]{1,0:T(8,128)(2,1)S(1)} custom-call(bf16[64,1152]{1,0:T(8,128)(2,1)S(1)} %collective-permute-done.3.child, bf16[2,2,64,64]{3,2,1,0:T(8,128)(2,1)S(1)} %get-tuple-element.13.mats, s32[2,2,64,128]{3,2,1,0:T(8,128)S(1)} %get-tuple-element.14.rows, f32[64,1152]{1,0:T(8,128)S(1)} %merge_own.2.partial), custom_call_target="tpu_custom_call" | custom-call | tf_op jit(solution)/shard_map/merge_other/pallas_call | solution.py:196
  18.6 2.8 %collective-permute-start.4 = (bf16[64,1152]{1,0:T(8,128)(2,1)S(1)}, bf16[64,1152]{1,0:T(8,128)(2,1)S(1)}, u32[]{:S(2)}, u32[]{:S(2)}) collective-permute-start(bf16[64,1152]{1,0:T(8,128)(2,1)S(1)} %merge_other.2.child), channel_id=1, source_target_pairs={{0,8},{4,12},{8,0},{12,4},{1,9},{5,13},{9,1},{13,5},{2,10},{6,14},... | collective-permute-start | bytes 442376 | tf_op jit(solution)/shard_map/ppermute | solution.py:282
  21.4 0.3 %merge_own.3.partial = f32[64,1152]{1,0:T(8,128)S(1)} custom-call(bf16[64,1152]{1,0:T(8,128)(2,1)S(1)} %merge_other.2.child, bf16[2,2,64,64]{3,2,1,0:T(8,128)(2,1)S(1)} %get-tuple-element.13.mats, s32[2,2,64,128]{3,2,1,0:T(8,128)S(1)} %get-tuple-element.14.rows), custom_call_target="tpu_custom_call" | custom-call | tf_op jit(solution)/shard_map/merge_own/pallas_call | solution.py:196
  21.7 6.1 %collective-permute-done.4.child = bf16[64,1152]{1,0:T(8,128)(2,1)S(1)} collective-permute-done((bf16[64,1152]{1,0:T(8,128)(2,1)S(1)}, bf16[64,1152]{1,0:T(8,128)(2,1)S(1)}, u32[]{:S(2)}, u32[]{:S(2)}) %collective-permute-start.4) | collective-permute-done | bytes 147488 | tf_op jit(solution)/shard_map/ppermute | solution.py:282
  27.9 1.0 %merge_other.3 = bf16[2,32,1024]{2,1,0:T(8,128)(2,1)} custom-call(bf16[64,1152]{1,0:T(8,128)(2,1)S(1)} %collective-permute-done.4.child, bf16[2,2,64,64]{3,2,1,0:T(8,128)(2,1)S(1)} %get-tuple-element.13.mats, s32[2,2,64,128]{3,2,1,0:T(8,128)S(1)} %get-tuple-element.14.rows, f32[64,1152]{1,0:T(8,128)S(1)} %merge_own.3.partial), custom_call_target="tpu_custom_call" | custom-call | tf_op jit(solution)/shard_map/merge_other/pallas_call | solution.py:196
Async XLA Ops:
  0.0 8.2 %copy-start = (bf16[2,64,1024]{2,1,0:T(8,128)(2,1)S(1)}, bf16[2,64,1024]{2,1,0:T(8,128)(2,1)}, u32[]{:S(2)}) copy-start(bf16[2,64,1024]{2,1,0:T(8,128)(2,1)} %echoes.1) | copy-start | bytes 786436
  0.0 4.0 %copy-start.1 = (f32[64,64]{1,0:T(8,128)S(1)}, f32[64,64]{1,0:T(8,128)}, u32[]{:S(2)}) copy-start(f32[64,64]{1,0:T(8,128)} %phase.1) | copy-start | bytes 49156
  0.0 4.0 %copy-start.2 = (s32[64,64]{1,0:T(8,128)S(1)}, s32[64,64]{1,0:T(8,128)}, u32[]{:S(2)}) copy-start(s32[64,64]{1,0:T(8,128)} %shift.1) | copy-start | bytes 49156
  0.0 4.0 %copy-start.5 = (bf16[2,512]{1,0:T(2,128)(2,1)S(1)}, bf16[2,512]{1,0:T(2,128)(2,1)}, u32[]{:S(2)}) copy-start(bf16[2,512]{1,0:T(2,128)(2,1)} %chirp.1) | copy-start | bytes 6148
  0.0 4.0 %copy-start.6 = (s32[2,2,32]{2,1,0:T(2,128)S(1)}, s32[2,2,32]{2,1,0:T(2,128)}, u32[]{:S(2)}) copy-start(s32[2,2,32]{2,1,0:T(2,128)} %mshift.1) | copy-start | bytes 1540
  1.0 7.2 %collective-permute-start.1 = (bf16[2,64,640]{2,1,0:T(8,128)(2,1)S(1)}, bf16[2,64,640]{2,1,0:T(8,128)(2,1)S(1)}, u32[]{:S(2)}, u32[]{:S(2)}) collective-permute-start(bf16[2,64,640]{2,1,0:T(8,128)(2,1)S(1)} %constant_dynamic-slice_fusion), channel_id=1, source_target_pairs={{0,2},{2,0},{1,3},{3,1},{4,6},{6,4},{5,7},{7,5},{8,10},{10,8},{9,1... | collective-permute-start | bytes 491528 | tf_op jit(solution)/shard_map/ppermute | solution.py:213
  4.1 0.8 %copy-start.3 = (f32[2,2,2,8,32]{4,3,2,1,0:T(8,128)S(1)}, f32[2,2,2,8,32]{4,3,2,1,0:T(8,128)}, u32[]{:S(2)}) copy-start(f32[2,2,2,8,32]{4,3,2,1,0:T(8,128)} %mweight.1) | copy-start | bytes 24580
  4.8 0.7 %copy-start.4 = (s32[2,2,8,32]{3,2,1,0:T(8,128)S(1)}, s32[2,2,8,32]{3,2,1,0:T(8,128)}, u32[]{:S(2)}) copy-start(s32[2,2,8,32]{3,2,1,0:T(8,128)} %taps.1) | copy-start | bytes 12292
  9.0 1.7 %collective-permute-start.2 = (bf16[128,1152]{1,0:T(8,128)(2,1)S(1)}, bf16[128,1152]{1,0:T(8,128)(2,1)S(1)}, u32[]{:S(2)}, u32[]{:S(2)}) collective-permute-start(bf16[128,1152]{1,0:T(8,128)(2,1)S(1)} %compress.1.mine), channel_id=1, source_target_pairs={{0,1},{1,0},{2,3},{3,2},{4,5},{5,4},{6,7},{7,6},{8,9},{9,8},{10,11... | collective-permute-start | bytes 884744 | tf_op jit(solution)/shard_map/ppermute | solution.py:265
  9.1 1.6 %collective-permute-start = (bf16[96,128]{1,0:T(8,128)(2,1)S(1)}, bf16[96,128]{1,0:T(8,128)(2,1)S(1)}, u32[]{:S(2)}, u32[]{:S(2)}) collective-permute-start(bf16[96,128]{1,0:T(8,128)(2,1)S(1)} %get-tuple-element.11), channel_id=1, source_target_pairs={{0,1},{1,0},{2,3},{3,2},{4,5},{5,4},{6,7},{7,6},{8,9},{9,8},{10,11... | collective-permute-start | bytes 73736 | tf_op jit(solution)/shard_map/ppermute | solution.py:257
  12.2 6.0 %collective-permute-start.3 = (bf16[64,1152]{1,0:T(8,128)(2,1)S(1)}, bf16[64,1152]{1,0:T(8,128)(2,1)S(1)}, u32[]{:S(2)}, u32[]{:S(2)}) collective-permute-start(bf16[64,1152]{1,0:T(8,128)(2,1)S(1)} %project.1.child), channel_id=1, source_target_pairs={{0,4},{4,0},{8,12},{12,8},{1,5},{5,1},{9,13},{13,9},{2,6},{6,2},{1... | collective-permute-start | bytes 442376 | tf_op jit(solution)/shard_map/ppermute | solution.py:282
  18.6 9.3 %collective-permute-start.4 = (bf16[64,1152]{1,0:T(8,128)(2,1)S(1)}, bf16[64,1152]{1,0:T(8,128)(2,1)S(1)}, u32[]{:S(2)}, u32[]{:S(2)}) collective-permute-start(bf16[64,1152]{1,0:T(8,128)(2,1)S(1)} %merge_other.2.child), channel_id=1, source_target_pairs={{0,8},{4,12},{8,0},{12,4},{1,9},{5,13},{9,1},{13,5},{2,10},{6,14},... | collective-permute-start | bytes 442376 | tf_op jit(solution)/shard_map/ppermute | solution.py:282
